TPU v7x, 32 devices: a whole 2x2x4 slice. The times are simulated.
32 devices in a mesh: dp: 8 (over z, y), mp: 4 (over x, core).
Axes of the slice: x: 2, y: 2, z: 4, core: 2. Of those that a mesh axis runs over, the one named last changes fastest.
Arguments:
- tokens: bfloat16 [16, 1024, 1024], P(None, ('dp', 'mp')), may hold values from -6 to 6
- encoder: bfloat16 [16, 1024, 1024], P(None, ('dp', 'mp')), may hold values from -6 to 6
- cotangent: bfloat16 [16, 1024, 1024], P(None, ('dp', 'mp')), may hold values from -6 to 6
- lengths: int32 [16], replicated, may hold values from 1 to 1024, 8192 in all
- deal: int32 [16], replicated, may hold values from 0 to 15, each once
- attn_in: float32 [6, 1024, 1024], P(None, 'dp', 'mp'), may hold values from -0.16 to 0.16
- attn_out: float32 [2, 1024, 1024], P(None, 'mp', 'dp'), may hold values from -0.75 to 0.75
- ff_in: float32 [2, 1024, 2816], P(None, 'dp', 'mp'), may hold values from -0.1875 to 0.1875
- ff_out: float32 [2816, 1024], P('mp', 'dp'), may hold values from -0.109375 to 0.109375
- gains: float32 [3, 1024], P(None, 'dp'), may hold values from 0.5 to 1.5
- mom_attn_in: float32 [6, 1024, 1024], P(None, 'dp', 'mp'), may hold values from -6 to 6
- mom_attn_out: float32 [2, 1024, 1024], P(None, 'mp', 'dp'), may hold values from -6 to 6
- mom_ff_in: float32 [2, 1024, 2816], P(None, 'dp', 'mp'), may hold values from -6 to 6
- mom_ff_out: float32 [2816, 1024], P('mp', 'dp'), may hold values from -6 to 6
- mom_gains: float32 [3, 1024], P(None, 'dp'), may hold values from -6 to 6
- avg_attn_in: float32 [6, 1024, 1024], P(None, 'dp', 'mp'), may hold values from -0.1875 to 0.1875
- avg_attn_out: float32 [2, 1024, 1024], P(None, 'mp', 'dp'), may hold values from -0.75 to 0.75
- avg_ff_in: float32 [2, 1024, 2816], P(None, 'dp', 'mp'), may hold values from -0.1875 to 0.1875
- avg_ff_out: float32 [2816, 1024], P('mp', 'dp'), may hold values from -0.109375 to 0.109375
- avg_gains: float32 [3, 1024], P(None, 'dp'), may hold values from 0.5 to 1.5
Outputs:
- block_output: float32 [16, 1024, 1024], P(None, ('dp', 'mp'))
- grad_tokens: float32 [16, 1024, 1024], P(None, ('dp', 'mp'))
- grad_encoder: float32 [16, 1024, 1024], P(None, ('dp', 'mp'))
- grad_attn_in: float32 [6, 1024, 1024], P(None, 'dp', 'mp')
- moment_attn_in: float32 [6, 1024, 1024], P(None, 'dp', 'mp')
- average_attn_in: float32 [6, 1024, 1024], P(None, 'dp', 'mp')
- master_attn_in: float32 [6, 1024, 1024], P(None, 'dp', 'mp')
- grad_attn_out: float32 [2, 1024, 1024], P(None, 'mp', 'dp')
- moment_attn_out: float32 [2, 1024, 1024], P(None, 'mp', 'dp')
- average_attn_out: float32 [2, 1024, 1024], P(None, 'mp', 'dp')
- master_attn_out: float32 [2, 1024, 1024], P(None, 'mp', 'dp')
- grad_ff_in: float32 [2, 1024, 2816], P(None, 'dp', 'mp')
- moment_ff_in: float32 [2, 1024, 2816], P(None, 'dp', 'mp')
- average_ff_in: float32 [2, 1024, 2816], P(None, 'dp', 'mp')
- master_ff_in: float32 [2, 1024, 2816], P(None, 'dp', 'mp')
- grad_ff_out: float32 [2816, 1024], P('mp', 'dp')
- moment_ff_out: float32 [2816, 1024], P('mp', 'dp')
- average_ff_out: float32 [2816, 1024], P('mp', 'dp')
- master_ff_out: float32 [2816, 1024], P('mp', 'dp')
- grad_gains: float32 [3, 1024], P(None, 'dp')
- moment_gains: float32 [3, 1024], P(None, 'dp')
- average_gains: float32 [3, 1024], P(None, 'dp')
- master_gains: float32 [3, 1024], P(None, 'dp')
- head_maxima: float32 [16], P('mp')
- clip_factors: float32 [16], P('mp')
Inputs may be any that keep to these rules, and one draw needn't show every extreme that they name: lengths[j] counts the real tokens of slot j; positions from lengths[j] on are padding. deal holds each slot once; slot j is micro-batch j % 2 of data index j // 2.
All inputs are finite; a program needn't handle non-finite values.
Results may differ from a plain program's by a relative error of at most 0.025.
The roundings to bfloat16 on the way count: a program that leaves them out, or rounds other values in their place, can miss the bound.
Values may be sent and summed in bfloat16 or wider, within the bound.
No kernel may reach another device: no remote copies, remote signals or barrier semaphores. Data moves between devices by JAX's collectives and lax.ppermute only.
A program may use at most 256 MiB of HBM per device.

v0:
```python
import jax
import jax.numpy as jnp
from jax import lax
from jax.sharding import Mesh, PartitionSpec as P

D = 1024
DK = 64
epsilon = 1e-06
clip_limit = 10.0
momentum_rate = 0.9
learn_rate = 0.01
average_rate = 0.5
neg_large = -1e30
bf16 = jnp.bfloat16
f32 = jnp.float32
swap = ((0, 1), (1, 0))
chips = ("dp", "mx")


def rms_norm(hidden, gain_vec):
    row_scale = lax.rsqrt(jnp.mean(hidden * hidden, axis=-1, keepdims=True) + epsilon)
    return hidden * row_scale * gain_vec


def gelu_product(gate_part, up_part):
    return jax.nn.gelu(gate_part, approximate=True) * up_part


def nn(left, right):
    return lax.dot_general(left, right, (((1,), (0,)), ((), ())), preferred_element_type=f32)


def nt(left, right):
    return lax.dot_general(left, right, (((1,), (1,)), ((), ())), preferred_element_type=f32)


def tn(left, right):
    return lax.dot_general(left, right, (((0,), (0,)), ((), ())), preferred_element_type=f32)


def both_cores(own):
    return jnp.concatenate([own, lax.ppermute(own, "mc", swap)], axis=0)


def sum_cores(parts):
    own, other = parts
    return own + lax.ppermute(other, "mc", swap)


def split_heads(values):
    return values.reshape(values.shape[0], values.shape[1] // DK, DK)


def attend(query, keys, values, allowed):
    query_h, keys_h, values_h = (split_heads(query), split_heads(keys), split_heads(values))
    scores = jnp.einsum("qhe,khe->hqk", query_h, keys_h, preferred_element_type=f32)
    masked = jnp.where(allowed, scores, neg_large)
    row_top = jnp.max(masked, axis=-1, keepdims=True)
    expo_rows = jnp.exp(masked - row_top)
    row_total = jnp.sum(expo_rows, axis=-1, keepdims=True)
    soft_rows = expo_rows / row_total
    mixed = jnp.einsum("hqk,khe->qhe", soft_rows.astype(bf16), values_h, preferred_element_type=f32)
    return (mixed.reshape(query.shape).astype(bf16), row_top + jnp.log(row_total), row_top)


def attend_back(query, keys, values, allowed, log_total, grad_mixed):
    query_h, keys_h, values_h = (split_heads(query), split_heads(keys), split_heads(values))
    grad_h = split_heads(grad_mixed)
    scores = jnp.einsum("qhe,khe->hqk", query_h, keys_h, preferred_element_type=f32)
    soft_rows = jnp.exp(jnp.where(allowed, scores, neg_large) - log_total)
    grad_soft = jnp.einsum("qhe,khe->hqk", grad_h, values_h, preferred_element_type=f32)
    grad_values = jnp.einsum(
        "hqk,qhe->khe", soft_rows.astype(bf16), grad_h, preferred_element_type=f32
    )
    row_dot = jnp.sum(grad_soft * soft_rows, axis=-1, keepdims=True)
    grad_scores = (soft_rows * (grad_soft - row_dot)).astype(bf16)
    grad_query = jnp.einsum("hqk,khe->qhe", grad_scores, keys_h, preferred_element_type=f32)
    grad_keys = jnp.einsum("hqk,qhe->khe", grad_scores, query_h, preferred_element_type=f32)
    return tuple(
        (t.reshape(t.shape[0], -1).astype(bf16) for t in (grad_query, grad_keys, grad_values))
    )


def norm_back(hidden, gain_vec, grad):
    row_scale = lax.rsqrt(jnp.mean(hidden * hidden, axis=-1, keepdims=True) + epsilon)
    z = hidden * row_scale
    grad_z = grad * gain_vec
    grad_hidden = row_scale * (grad_z - z * jnp.mean(grad_z * z, axis=-1, keepdims=True))
    return (grad_hidden, jnp.sum(grad * z, axis=0))


def apply_update(weight, grad_sum, moment, average, factor, grad_scale):
    grad_now = grad_sum * grad_scale
    moment_new = momentum_rate * moment + grad_now
    master_new = (weight - learn_rate * (grad_now + momentum_rate * moment_new)) * factor
    average_new = average_rate * average + (1.0 - average_rate) * master_new
    return (grad_now, moment_new, average_new, master_new)


def flat_columns(block):
    return jnp.swapaxes(block, 0, 1).reshape(block.shape[1], -1)


def gather_chunk(local):
    own = lax.all_gather(local, "dp", axis=0, tiled=True)
    return (own, lax.ppermute(own, "mx", swap))


def reduce_chunk(own, other):
    arrived = lax.ppermute(other.astype(bf16), "mx", swap)
    total = (own + arrived.astype(f32)).astype(bf16)
    return lax.psum_scatter(total, "dp", scatter_dimension=0, tiled=True).astype(f32)


def on_device(
    tokens,
    encoder,
    cotangent,
    lengths,
    deal,
    attn_in,
    attn_out,
    ff_in,
    ff_out,
    gains,
    mom_attn_in,
    mom_attn_out,
    mom_ff_in,
    mom_ff_out,
    mom_gains,
    avg_attn_in,
    avg_attn_out,
    avg_ff_in,
    avg_ff_out,
    avg_gains,
):
    seq_count, block_rows = (tokens.shape[0], tokens.shape[1])
    core = lax.axis_index("mc")
    chip = lax.axis_index("dp") * lax.axis_size("mx") + lax.axis_index("mx")
    own_rows = block_rows * seq_count
    slot_len = 2 * own_rows
    heads_cols = attn_in.shape[2]
    hidden = ff_in.shape[2]
    model_rows = attn_in.shape[1]

    def to_chips(values):
        moved = lax.all_to_all(values, chips, split_axis=0, concat_axis=1, tiled=True)
        return moved.reshape(own_rows, D)

    def from_chips(rows):
        return lax.all_to_all(
            rows.reshape(1, own_rows, D), chips, split_axis=1, concat_axis=0, tiled=True
        ).astype(f32)

    seq_len = lengths[deal[chip]]
    row_ids = jnp.arange(own_rows, dtype=jnp.int32)
    lane = row_ids % block_rows
    pos_own = (row_ids // block_rows * 2 + core) * block_rows + lane
    pos_other = (row_ids // block_rows * 2 + 1 - core) * block_rows + lane
    pos = jnp.concatenate([pos_own, pos_other])
    allowed = pos[None, :] <= pos[:, None]
    valid_own = (pos_own < seq_len).astype(f32)[:, None]
    valid_all = pos < seq_len
    pad = jnp.zeros((model_rows, 125), bf16)
    chunk_a = jnp.concatenate(
        [flat_columns(attn_in[0:3].astype(bf16)), gains.astype(bf16).T, pad], axis=1
    )
    out_t = jnp.swapaxes(attn_out.astype(bf16), 1, 2)
    chunk_b = jnp.concatenate([out_t[0], flat_columns(attn_in[3:6].astype(bf16)), out_t[1]], axis=1)
    chunk_c = flat_columns(ff_in.astype(bf16))
    chunk_d = ff_out.astype(bf16).T
    tok_own = to_chips(tokens)
    got_a = gather_chunk(chunk_a)
    enc_own = to_chips(encoder)
    got_b = gather_chunk(chunk_b)
    cot_own = to_chips(cotangent)
    got_c = gather_chunk(chunk_c)
    got_d = gather_chunk(chunk_d)
    gain_f = got_a[0][:, 3 * heads_cols : 3 * heads_cols + 3].astype(f32).T
    hc = heads_cols
    w_qkv = [g[:, : 3 * hc] for g in got_a]
    w_ot = [g[:, :hc] for g in got_b]
    w_cq = [g[:, hc : 2 * hc] for g in got_b]
    w_ckv = [g[:, 2 * hc : 4 * hc] for g in got_b]
    w_cot = [g[:, 4 * hc :] for g in got_b]
    w_gu = got_c
    w_dt = got_d
    halves = lambda v: (v[:own_rows], v[own_rows:])
    x_rows = tok_own.astype(f32)
    norm_one = both_cores(rms_norm(x_rows, gain_f[0]).astype(bf16))
    qkv = [nn(norm_one, w).astype(bf16) for w in w_qkv]
    qkv = [(t[:, :hc], t[:, hc : 2 * hc], t[:, 2 * hc :]) for t in qkv]
    self_out = [attend(q, k, v, allowed) for q, k, v in qkv]
    head_top = jnp.stack(
        [
            jnp.max(jnp.where(valid_all[None, :, None], o[2], neg_large), axis=(1, 2))
            for o in self_out
        ]
    )
    branch = nt(self_out[0][0], w_ot[0]) + nt(self_out[1][0], w_ot[1])
    hidden_one = x_rows + sum_cores(halves(branch))
    norm_two = both_cores(rms_norm(hidden_one, gain_f[1]).astype(bf16))
    enc_all = both_cores(enc_own)
    cross_q = [nn(norm_two, w).astype(bf16) for w in w_cq]
    cross_kv = [nn(enc_all, w).astype(bf16) for w in w_ckv]
    cross_kv = [(t[:, :hc], t[:, hc:]) for t in cross_kv]
    cross_out = [attend(q, k, v, True) for q, (k, v) in zip(cross_q, cross_kv)]
    branch = nt(cross_out[0][0], w_cot[0]) + nt(cross_out[1][0], w_cot[1])
    hidden_two = hidden_one + sum_cores(halves(branch))
    norm_three = both_cores(rms_norm(hidden_two, gain_f[2]).astype(bf16))
    gate_up = [nn(norm_three, w) for w in w_gu]
    gate_up = [(t[:, :hidden], t[:, hidden:]) for t in gate_up]
    inner = [gelu_product(g, u).astype(bf16) for g, u in gate_up]
    branch = nt(inner[0], w_dt[0]) + nt(inner[1], w_dt[1])
    out_rows = (hidden_two + sum_cores(halves(branch))) * valid_own
    block_output = from_chips(out_rows.astype(bf16))
    grad_out = cot_own.astype(f32) * valid_own
    grad_out_all = both_cores(grad_out.astype(bf16))
    g_dt = [tn(grad_out_all, f) for f in inner]
    red_d = reduce_chunk(*g_dt)
    grad_gu = []
    for (g, u), w in zip(gate_up, w_dt):
        _, back = jax.vjp(gelu_product, g, u)
        dg, du = back(nn(grad_out_all, w))
        grad_gu.append(jnp.concatenate([dg.astype(bf16), du.astype(bf16)], axis=1))
    g_gu = [tn(norm_three, t) for t in grad_gu]
    red_c = reduce_chunk(*g_gu)
    grad_norm = sum_cores(halves(nt(grad_gu[0], w_gu[0]) + nt(grad_gu[1], w_gu[1])))
    grad_h, gain_three = norm_back(hidden_two, gain_f[2], grad_norm)
    grad_hidden_two = grad_out + grad_h
    grad_co = both_cores(grad_hidden_two.astype(bf16))
    g_cot = [tn(grad_co, o[0]) for o in cross_out]
    grad_ca = [nn(grad_co, w).astype(bf16) for w in w_cot]
    cross_back = [
        attend_back(q, k, v, True, o[1], d)
        for q, (k, v), o, d in zip(cross_q, cross_kv, cross_out, grad_ca)
    ]
    g_cq = [tn(norm_two, b[0]) for b in cross_back]
    d_ckv = [jnp.concatenate([b[1], b[2]], axis=1) for b in cross_back]
    g_ckv = [tn(enc_all, t) for t in d_ckv]
    red_b = reduce_chunk(*[jnp.concatenate(t, axis=1) for t in zip(g_cq, g_ckv, g_cot)])
    grad_norm = sum_cores(halves(nt(cross_back[0][0], w_cq[0]) + nt(cross_back[1][0], w_cq[1])))
    grad_enc = sum_cores(halves(nt(d_ckv[0], w_ckv[0]) + nt(d_ckv[1], w_ckv[1])))
    grad_encoder = from_chips(grad_enc.astype(bf16))
    grad_h, gain_two = norm_back(hidden_one, gain_f[1], grad_norm)
    grad_hidden_one = grad_hidden_two + grad_h
    grad_o = both_cores(grad_hidden_one.astype(bf16))
    g_ot = [tn(grad_o, o[0]) for o in self_out]
    grad_a = [nn(grad_o, w).astype(bf16) for w in w_ot]
    self_back = [
        jnp.concatenate(attend_back(q, k, v, allowed, o[1], d), axis=1)
        for (q, k, v), o, d in zip(qkv, self_out, grad_a)
    ]
    g_qkv = [tn(norm_one, t) for t in self_back]
    red_a = reduce_chunk(*[jnp.concatenate(t, axis=1) for t in zip(g_qkv, g_ot)])
    grad_norm = sum_cores(halves(nt(self_back[0], w_qkv[0]) + nt(self_back[1], w_qkv[1])))
    grad_h, gain_one = norm_back(x_rows, gain_f[0], grad_norm)
    grad_tokens = from_chips((grad_hidden_one + grad_h).astype(bf16))
    gain_total = lax.psum(jnp.stack([gain_one, gain_two, gain_three]), ("mx", "mc"))
    red_gain = lax.psum_scatter(gain_total, "dp", scatter_dimension=1, tiled=True)
    mx = lax.axis_index("mx")
    local_heads = hc // DK
    head_rows = jnp.where(mx == 0, head_top, head_top[::-1])
    head_peak = lax.dynamic_index_in_dim(lax.pmax(head_rows, chips), mx, 0, keepdims=False)
    unflat = lambda t, n: jnp.swapaxes(t.reshape(model_rows, n, -1), 0, 1)
    red_in = jnp.concatenate([unflat(red_a[:, : 3 * hc], 3), unflat(red_b[:, : 3 * hc], 3)])
    red_out = jnp.stack([red_a[:, 3 * hc :].T, red_b[:, 3 * hc :].T])
    clip_factors = clip_limit / jnp.maximum(head_peak, clip_limit)
    column = jnp.repeat(jnp.sqrt(clip_factors), DK)
    factor = jnp.where((jnp.arange(6) < 2)[:, None, None], column[None, None, :], 1.0)
    grad_scale = float(seq_count * slot_len) ** (-0.5)
    up_a = apply_update(attn_in, red_in, mom_attn_in, avg_attn_in, factor, grad_scale)
    up_b = apply_update(attn_out, red_out, mom_attn_out, avg_attn_out, 1.0, grad_scale)
    up_c = apply_update(ff_in, unflat(red_c, 2), mom_ff_in, avg_ff_in, 1.0, grad_scale)
    up_d = apply_update(ff_out, red_d.T, mom_ff_out, avg_ff_out, 1.0, grad_scale)
    up_e = apply_update(gains, red_gain, mom_gains, avg_gains, 1.0, grad_scale)
    return (
        block_output,
        grad_tokens,
        grad_encoder,
        *up_a,
        *up_b,
        *up_c,
        *up_d,
        *up_e,
        head_peak,
        clip_factors,
    )


def solution(mesh):
    dp, mp = (mesh.shape["dp"], mesh.shape["mp"])
    fine = Mesh(mesh.devices.reshape(dp, mp // 2, 2), ("dp", "mx", "mc"))
    mp_axes = ("mx", "mc")
    rows = P(None, ("dp", "mx", "mc"), None)
    wide = P(None, "dp", mp_axes)
    tall = P(None, mp_axes, "dp")
    down = P(mp_axes, "dp")
    gain = P(None, "dp")
    state = (wide, tall, wide, down, gain)
    in_specs = (rows, rows, rows, P(), P(), *state, *state, *state)
    out_specs = (
        rows,
        rows,
        rows,
        *[wide] * 4,
        *[tall] * 4,
        *[wide] * 4,
        *[down] * 4,
        *[gain] * 4,
        P(mp_axes),
        P(mp_axes),
    )
    return jax.shard_map(
        on_device, mesh=fine, in_specs=in_specs, out_specs=out_specs, check_vma=False
    )
```

profile of v0, /device:TPU:0, one launch (start us, length us, event | category | flops | bytes accessed | tf_op | source)
XLA Modules:
  0.0 978.8 jit_solution(4755610367959535407)
XLA Ops:
  10.4 8.3 all-to-all-start
  19.6 30.9 %all-to-all-done = bf16[16,32,1024]{2,1,0:T(8,128)(2,1)S(1)} async-done(((bf16[16,32,1024]{2,1,0:T(8,128)(2,1)}), bf16[16,32,1024]{2,1,0:T(8,128)(2,1)S(1)}, u32[]{:S(2)}, u32[]{:S(2)}) %all-to-all-start) | async-done | bytes 1048608 | tf_op jit(solution)/shard_map/all_to_all | solution.py:147
  50.9 20.9 %all-gather.5.cloned.1.call-done = bf16[1024,896]{0,1:T(8,128)(2,1)} async-done(((bf16[128,896]{0,1:T(8,128)(2,1)}), bf16[1024,896]{0,1:T(8,128)(2,1)}) %all-gather.5.cloned.1.call-update) | async-done | bytes 1835024 | tf_op jit(solution)/shard_map/all_gather | solution.py:105
  81.4 8.2 fusion.153
  89.6 39.9 %all-gather.7.cloned.1.call-done = bf16[1024,1280]{0,1:T(8,128)(2,1)} async-done(((bf16[128,1280]{0,1:T(8,128)(2,1)}), bf16[1024,1280]{0,1:T(8,128)(2,1)}) %all-gather.7.cloned.1.call-update) | async-done | bytes 2621456 | tf_op jit(solution)/shard_map/all_gather | solution.py:105
  138.4 9.9 %select_reduce_fusion = (f32[4,1024]{1,0:T(4,128)}, f32[4,1024]{1,0:T(4,128)}, f32[4,1024,1024]{1,2,0:T(8,128)}) fusion(pred[1024,1024]{0,1:T(8,128)(4,1)S(1)} %broadcast_compare_fusion, f32[4,1024,1024]{1,2,0:T(8,128)S(1)} %copy-done, bf16[1024,4,64]{0,2,1:T(8,128)(2,1)} %bitcast.269, bf16[1024,4,64]{0,2,1:T(8,128)(2,1)} %bitcast.267), kind=kOutput, calls=%fused_computation.24 | convolution fusion | flops 553639936 | bytes 35684352 | tf_op jit(solution)/shard_map/qhe,khe->hqk/dot_general | solution.py:56
  148.3 9.1 fusion.1
  164.0 8.2 fusion.78
  172.2 15.8 %collective-permute-done.2 = bf16[1024,1280]{0,1:T(8,128)(2,1)} collective-permute-done((bf16[1024,1280]{0,1:T(8,128)(2,1)}, bf16[1024,1280]{0,1:T(8,128)(2,1)}, u32[]{:S(2)}, u32[]{:S(2)}) %collective-permute-start.2) | collective-permute-done | bytes 2621472 | tf_op jit(solution)/shard_map/ppermute | solution.py:106
  191.9 30.0 %all_to_all.24 = bf16[16,32,1024]{2,1,0:T(8,128)(2,1)} all-to-all(bf16[16,32,1024]{2,1,0:T(8,128)(2,1)S(1)} %copy-done.58), channel_id=1, replica_groups=mesh['dp'=8,'mx'=2,'mc'=2] {'dp','mx'}, dimensions={0} | all-to-all | bytes 2097152 | tf_op jit(solution)/shard_map/all_to_all | solution.py:147
  235.7 8.2 fusion.151
  243.9 8.0 fusion.2
  262.1 8.2 fusion.152
  312.1 19.2 %all-to-all-done.3 = bf16[16,32,1024]{2,1,0:T(8,128)(2,1)} async-done(((bf16[16,32,1024]{2,1,0:T(8,128)(2,1)}), bf16[16,32,1024]{2,1,0:T(8,128)(2,1)}, u32[]{:S(2)}, u32[]{:S(2)}) %all-to-all-start.3) | async-done | bytes 1048608 | tf_op jit(solution)/shard_map/all_to_all | solution.py:147
  333.8 15.6 %all-gather.11.cloned.1.call-done = bf16[1024,704]{0,1:T(8,128)(2,1)} async-done(((bf16[128,704]{0,1:T(8,128)(2,1)}), bf16[1024,704]{0,1:T(8,128)(2,1)}) %all-gather.11.cloned.1.call-update) | async-done | bytes 1441808 | tf_op jit(solution)/shard_map/all_gather | solution.py:105
  356.8 20.6 %collective-permute-done.8 = bf16[1024,1408]{0,1:T(8,128)(2,1)} collective-permute-done((bf16[1024,1408]{0,1:T(8,128)(2,1)}, bf16[1024,1408]{0,1:T(8,128)(2,1)}, u32[]{:S(2)}, u32[]{:S(2)}) %collective-permute-start.8) | collective-permute-done | bytes 2883616 | tf_op jit(solution)/shard_map/ppermute | solution.py:106
  388.7 18.6 %collective-permute-done.9 = bf16[1024,704]{0,1:T(8,128)(2,1)S(1)} collective-permute-done((bf16[1024,704]{0,1:T(8,128)(2,1)}, bf16[1024,704]{0,1:T(8,128)(2,1)S(1)}, u32[]{:S(2)}, u32[]{:S(2)}) %collective-permute-start.9) | collective-permute-done | bytes 1441824 | tf_op jit(solution)/shard_map/ppermute | solution.py:106
  440.0 11.2 %multiply_reduce_fusion.3 = (f32[4,1024]{1,0:T(4,128)}, f32[4,1024,1024]{1,2,0:T(8,128)}) fusion(f32[4,1024,1024]{1,2,0:T(8,128)S(1)} %bitcast.246, f32[4,1024]{1,0:T(4,128)S(1)} %log_add_fusion.3, bf16[1024,4,64]{0,2,1:T(8,128)(2,1)} %bitcast.282, bf16[1024,4,64]{0,2,1:T(8,128)(2,1)} %bitcast.291), kind=kOutput, calls=%fused_computation.10 | convolution fusion | flops 549449728 | bytes 34635776 | tf_op jit(solution)/shard_map/qhe,khe->hqk/dot_general | solution.py:71
  465.6 16.2 %multiply_reduce_fusion.2 = (f32[4,1024]{1,0:T(4,128)}, f32[4,1024,1024]{1,2,0:T(8,128)}) fusion(f32[4,1024,1024]{1,2,0:T(8,128)} %get-tuple-element.99, f32[4,1024]{1,0:T(4,128)S(1)} %copy-done.85, bf16[1024,4,64]{0,2,1:T(8,128)(2,1)} %bitcast.284, bf16[1024,4,64]{0,2,1:T(8,128)(2,1)} %bitcast.289), kind=kOutput, calls=%fused_computation.7 | convolution fusion | flops 549449728 | bytes 34635776 | tf_op jit(solution)/shard_map/qhe,khe->hqk/dot_general | solution.py:71
  481.7 8.1 multiply_convert_fusion.2
  514.9 21.3 %collective-permute-done.21 = bf16[1024,704]{0,1:T(8,128)(2,1)S(1)} collective-permute-done((bf16[1024,704]{0,1:T(8,128)(2,1)S(1)}, bf16[1024,704]{0,1:T(8,128)(2,1)S(1)}, u32[]{:S(2)}, u32[]{:S(2)}) %collective-permute-start.21) | collective-permute-done | bytes 1441824 | tf_op jit(solution)/shard_map/ppermute | solution.py:110
  543.9 8.3 fusion.155
  570.9 24.6 %multiply_reduce_fusion = (f32[4,1024]{1,0:T(4,128)S(1)}, f32[4,1024]{1,0:T(4,128)S(1)}, f32[4,1024,1024]{1,2,0:T(8,128)}) fusion(f32[4,1024,1024]{1,2,0:T(8,128)} %get-tuple-element.95, f32[4,1024]{1,0:T(4,128)S(1)} %log_add_fusion, pred[1024,1024]{0,1:T(8,128)(4,1)S(1)} %copy-done.4, f32[4,1024,1024]{1,2,0:T(8,128)} %fusion.155, ...), kind=kOutput, calls=%fused_computation.1 | convolution fusion | flops 570417152 | bytes 69271552 | tf_op jit(solution)/shard_map/qhe,khe->hqk/dot_general | solution.py:71
  595.6 29.9 %multiply_convert_fusion = (bf16[4,1024,1024]{1,2,0:T(8,128)(2,1)}, bf16[4,1024,1024]{1,2,0:T(8,128)(2,1)}) fusion(f32[4,1024,1024]{1,2,0:T(8,128)} %get-tuple-element.104, f32[4,1024,1024]{1,2,0:T(8,128)} %get-tuple-element.95, f32[4,1024]{1,0:T(4,128)S(1)} %get-tuple-element.31, f32[4,1024]{1,0:T(4,128)S(1)} %log_add_fusion, ...), kind=kLoop, calls=%fused_computation | loop fusion | flops 41943040 | bytes 85000192 | tf_op jit(solution)/shard_map/convert_element_type | solution.py:76
  653.9 8.1 add_convert_fusion
  669.1 8.8 fusion.75
  700.7 32.4 %collective-permute-done.19 = bf16[1024,1024]{0,1:T(8,128)(2,1)} collective-permute-done((bf16[1024,1024]{0,1:T(8,128)(2,1)}, bf16[1024,1024]{0,1:T(8,128)(2,1)}, u32[]{:S(2)}, u32[]{:S(2)}) %collective-permute-start.19) | collective-permute-done | bytes 2097184 | tf_op jit(solution)/shard_map/ppermute | solution.py:110
  779.7 22.5 %collective-permute-done.18 = bf16[1024,1024]{0,1:T(8,128)(2,1)} collective-permute-done((bf16[1024,1024]{0,1:T(8,128)(2,1)}, bf16[1024,1024]{0,1:T(8,128)(2,1)}, u32[]{:S(2)}, u32[]{:S(2)}) %collective-permute-start.18) | collective-permute-done | bytes 2097184 | tf_op jit(solution)/shard_map/ppermute | solution.py:110
  812.8 9.2 reduce.6
  843.0 15.5 %all-to-all-done.5 = bf16[16,2,16384]{2,1,0:T(2,128)(2,1)} async-done(((bf16[16,2,16384]{2,1,0:T(2,128)(2,1)}), bf16[16,2,16384]{2,1,0:T(2,128)(2,1)}, u32[]{:S(2)}, u32[]{:S(2)}) %all-to-all-start.5) | async-done | bytes 1048608 | tf_op jit(solution)/shard_map/all_to_all | solution.py:151
  865.4 57.6 %pmax.7 = f32[2,4]{1,0:T(2,128)S(1)} all-reduce(f32[2,4]{1,0:T(2,128)S(1)} %broadcast_select_fusion.1), channel_id=1, replica_groups=mesh['dp'=8,'mx'=2,'mc'=2] {'dp','mx'}, use_global_device_ids=true, to_apply=%region_22.23 | all-reduce | flops 8 | bytes 64 | tf_op jit(solution)/shard_map/pmax | solution.py:264
  956.5 8.9 reduce-scatter.16.cloned.1.call-done
  (569 shorter events, 397.9 us)
Async XLA Ops:
  7.2 64.6 %all-gather.5.cloned.1.call-start = ((), (), s32[]{:S(2)}) async-start(), calls=%async_computation.11 | async-start | bytes 2064384 | tf_op jit(solution)/shard_map/all_gather | solution.py:105
  10.4 40.1 %all-to-all-start = ((bf16[16,32,1024]{2,1,0:T(8,128)(2,1)}), bf16[16,32,1024]{2,1,0:T(8,128)(2,1)S(1)}, u32[]{:S(2)}, u32[]{:S(2)}) async-start(bf16[16,32,1024]{2,1,0:T(8,128)(2,1)} %param.20), calls=%async_computation | async-start | bytes 2097152 | tf_op jit(solution)/shard_map/all_to_all | solution.py:147
  18.7 110.8 %all-gather.7.cloned.1.call-start = ((), (), s32[]{:S(2)}) async-start(), calls=%async_computation.12 | async-start | bytes 2949120 | tf_op jit(solution)/shard_map/all_gather | solution.py:105
  19.6 281.5 %all-gather.9.cloned.1.call-start = ((), (), s32[]{:S(2)}) async-start(), calls=%async_computation.13 | async-start | bytes 3244032 | tf_op jit(solution)/shard_map/all_gather | solution.py:105
  74.1 56.9 %collective-permute-start.1 = (bf16[1024,896]{0,1:T(8,128)(2,1)}, bf16[1024,896]{0,1:T(8,128)(2,1)}, u32[]{:S(2)}, u32[]{:S(2)}) collective-permute-start(bf16[1024,896]{0,1:T(8,128)(2,1)} %all-gather.5.cloned.1.call-done), channel_id=1, source_target_pairs={{0,2},{2,0},{1,3},{3,1},{4,6},{6,4},{5,7},{7,5},{8,10},{10,8},{9,1... | collective-permute-start | bytes 5505032 | tf_op jit(solution)/shard_map/ppermute | solution.py:106
  129.5 58.5 %collective-permute-start.2 = (bf16[1024,1280]{0,1:T(8,128)(2,1)}, bf16[1024,1280]{0,1:T(8,128)(2,1)}, u32[]{:S(2)}, u32[]{:S(2)}) collective-permute-start(bf16[1024,1280]{0,1:T(8,128)(2,1)} %all-gather.7.cloned.1.call-done), channel_id=1, source_target_pairs={{0,2},{2,0},{1,3},{3,1},{4,6},{6,4},{5,7},{7,5},{8,10},{10,8},{9,1... | collective-permute-start | bytes 7864328 | tf_op jit(solution)/shard_map/ppermute | solution.py:106
  190.0 32.9 %collective-permute-start.3 = (f32[512,1024]{1,0:T(8,128)S(1)}, f32[512,1024]{1,0:T(8,128)}, u32[]{:S(2)}, u32[]{:S(2)}) collective-permute-start(f32[512,1024]{1,0:T(8,128)S(1)} %slice.222), channel_id=1, source_target_pairs={{0,1},{1,0},{2,3},{3,2},{4,5},{5,4},{6,7},{7,6},{8,9},{9,8},{10,11... | collective-permute-start | bytes 6291464 | tf_op jit(solution)/shard_map/ppermute | solution.py:47
  221.9 4.9 collective-permute-start.4
  222.7 126.7 %all-gather.11.cloned.1.call-start = ((), (), s32[]{:S(2)}) async-start(), calls=%async_computation.14 | async-start | bytes 1622016 | tf_op jit(solution)/shard_map/all_gather | solution.py:105
  226.2 8.5 collective-permute-start.5
  295.3 7.6 collective-permute-start.6
  296.5 34.8 %all-to-all-start.3 = ((bf16[16,32,1024]{2,1,0:T(8,128)(2,1)}), bf16[16,32,1024]{2,1,0:T(8,128)(2,1)}, u32[]{:S(2)}, u32[]{:S(2)}) async-start(bf16[16,32,1024]{2,1,0:T(8,128)(2,1)} %param.22), calls=%async_computation.3 | async-start | bytes 2097152 | tf_op jit(solution)/shard_map/all_to_all | solution.py:147
  300.8 629.1 %reduce-scatter.20.cloned.1.call-start = ((), (), s32[]{:S(2)}) async-start(), calls=%async_computation.18 | async-start | bytes 1769472
  301.1 76.3 %collective-permute-start.8 = (bf16[1024,1408]{0,1:T(8,128)(2,1)}, bf16[1024,1408]{0,1:T(8,128)(2,1)}, u32[]{:S(2)}, u32[]{:S(2)}) collective-permute-start(bf16[1024,1408]{0,1:T(8,128)(2,1)} %all-gather.9.cloned.1.call-done), channel_id=1, source_target_pairs={{0,2},{2,0},{1,3},{3,1},{4,6},{6,4},{5,7},{7,5},{8,10},{10,8},{9,1... | collective-permute-start | bytes 8650760 | tf_op jit(solution)/shard_map/ppermute | solution.py:106
  308.3 42.6 %collective-permute-start.7 = (bf16[512,1024]{1,0:T(8,128)(2,1)}, bf16[512,1024]{1,0:T(8,128)(2,1)}, u32[]{:S(2)}, u32[]{:S(2)}) collective-permute-start(bf16[512,1024]{1,0:T(8,128)(2,1)} %multiply_convert_fusion.8), channel_id=1, source_target_pairs={{0,1},{1,0},{2,3},{3,2},{4,5},{5,4},{6,7},{7,6},{8,9},{9,8},{10,11... | collective-permute-start | bytes 3145736 | tf_op jit(solution)/shard_map/ppermute | solution.py:42
  333.8 49.6 %collective-permute-start.11 = (bf16[512,1024]{1,0:T(8,128)(2,1)}, bf16[512,1024]{1,0:T(8,128)(2,1)}, u32[]{:S(2)}, u32[]{:S(2)}) collective-permute-start(bf16[512,1024]{1,0:T(8,128)(2,1)} %fusion.47), channel_id=1, source_target_pairs={{0,1},{1,0},{2,3},{3,2},{4,5},{5,4},{6,7},{7,6},{8,9},{9,8},{10,11... | collective-permute-start | bytes 3145736 | tf_op jit(solution)/shard_map/ppermute | solution.py:42
  349.4 57.9 %collective-permute-start.9 = (bf16[1024,704]{0,1:T(8,128)(2,1)}, bf16[1024,704]{0,1:T(8,128)(2,1)S(1)}, u32[]{:S(2)}, u32[]{:S(2)}) collective-permute-start(bf16[1024,704]{0,1:T(8,128)(2,1)} %all-gather.11.cloned.1.call-done), channel_id=1, source_target_pairs={{0,2},{2,0},{1,3},{3,1},{4,6},{6,4},{5,7},{7,5},{8,10},{10,8},{9,1... | collective-permute-start | bytes 4325384 | tf_op jit(solution)/shard_map/ppermute | solution.py:106
  421.9 4.6 collective-permute-start.12
  497.3 5.0 collective-permute-start.14
  501.7 34.5 %collective-permute-start.21 = (bf16[1024,704]{0,1:T(8,128)(2,1)S(1)}, bf16[1024,704]{0,1:T(8,128)(2,1)S(1)}, u32[]{:S(2)}, u32[]{:S(2)}) collective-permute-start(bf16[1024,704]{0,1:T(8,128)(2,1)S(1)} %convolution_convert_fusion.4), channel_id=1, source_target_pairs={{0,2},{2,0},{1,3},{3,1},{4,6},{6,4},{5,7},{7,5},{8,10},{10,8},{9,1... | collective-permute-start | bytes 4325384 | tf_op jit(solution)/shard_map/ppermute | solution.py:110
  505.6 35.8 %collective-permute-start.15 = (bf16[512,1024]{1,0:T(8,128)(2,1)}, bf16[512,1024]{1,0:T(8,128)(2,1)S(1)}, u32[]{:S(2)}, u32[]{:S(2)}) collective-permute-start(bf16[512,1024]{1,0:T(8,128)(2,1)} %get-tuple-element.61), channel_id=1, source_target_pairs={{0,1},{1,0},{2,3},{3,2},{4,5},{5,4},{6,7},{7,6},{8,9},{9,8},{10,11... | collective-permute-start | bytes 3145736 | tf_op jit(solution)/shard_map/ppermute | solution.py:42
  513.7 140.2 %collective-permute-start.20 = (bf16[1024,1408]{1,0:T(8,128)(2,1)}, bf16[1024,1408]{1,0:T(8,128)(2,1)}, u32[]{:S(2)}, u32[]{:S(2)}) collective-permute-start(bf16[1024,1408]{1,0:T(8,128)(2,1)} %convolution_convert_fusion), channel_id=1, source_target_pairs={{0,2},{2,0},{1,3},{3,1},{4,6},{6,4},{5,7},{7,5},{8,10},{10,8},{9,1... | collective-permute-start | bytes 8650760 | tf_op jit(solution)/shard_map/ppermute | solution.py:110
  541.1 398.4 %reduce-scatter.22.cloned.1.call-start = ((), (), s32[]{:S(2)}) async-start(), calls=%async_computation.19 | async-start | bytes 589824
  653.6 293.3 %reduce-scatter.14.cloned.1.call-start = ((), (), s32[]{:S(2)}) async-start(), calls=%async_computation.15 | async-start | bytes 3244032 | tf_op jit(solution)/shard_map/reduce_scatter | solution.py:112
  662.0 289.6 %reduce-scatter.18.cloned.1.call-start = ((), (), s32[]{:S(2)}) async-start(), calls=%async_computation.17 | async-start | bytes 2359296
  685.2 48.0 %collective-permute-start.19 = (bf16[1024,1024]{0,1:T(8,128)(2,1)}, bf16[1024,1024]{0,1:T(8,128)(2,1)}, u32[]{:S(2)}, u32[]{:S(2)}) collective-permute-start(bf16[1024,1024]{0,1:T(8,128)(2,1)} %pad_maximum_fusion.10), channel_id=1, source_target_pairs={{0,2},{2,0},{1,3},{3,1},{4,6},{6,4},{5,7},{7,5},{8,10},{10,8},{9,1... | collective-permute-start | bytes 6291464 | tf_op jit(solution)/shard_map/ppermute | solution.py:110
  748.0 54.2 %collective-permute-start.18 = (bf16[1024,1024]{0,1:T(8,128)(2,1)}, bf16[1024,1024]{0,1:T(8,128)(2,1)}, u32[]{:S(2)}, u32[]{:S(2)}) collective-permute-start(bf16[1024,1024]{0,1:T(8,128)(2,1)} %pad_maximum_fusion.9), channel_id=1, source_target_pairs={{0,2},{2,0},{1,3},{3,1},{4,6},{6,4},{5,7},{7,5},{8,10},{10,8},{9,1... | collective-permute-start | bytes 6291464 | tf_op jit(solution)/shard_map/ppermute | solution.py:110
  754.7 52.6 %collective-permute-start.17 = (f32[512,1024]{1,0:T(8,128)}, f32[512,1024]{1,0:T(8,128)}, u32[]{:S(2)}, u32[]{:S(2)}) collective-permute-start(f32[512,1024]{1,0:T(8,128)} %slice.250), channel_id=1, source_target_pairs={{0,1},{1,0},{2,3},{3,2},{4,5},{5,4},{6,7},{7,6},{8,9},{9,8},{10,11... | collective-permute-start | bytes 6291464 | tf_op jit(solution)/shard_map/ppermute | solution.py:47
  767.6 56.9 %all-to-all-start.2 = ((bf16[16,2,16384]{2,1,0:T(2,128)(2,1)}), bf16[16,2,16384]{2,1,0:T(2,128)(2,1)}, u32[]{:S(2)}, u32[]{:S(2)}) async-start(bf16[16,2,16384]{2,1,0:T(2,128)(2,1)} %reshape.470), calls=%async_computation.2 | async-start | bytes 2097152 | tf_op jit(solution)/shard_map/all_to_all | solution.py:151
  774.2 191.2 %reduce-scatter.16.cloned.1.call-start = ((), (), s32[]{:S(2)}) async-start(), calls=%async_computation.16 | async-start | bytes 2359296
  824.6 33.9 %all-to-all-start.5 = ((bf16[16,2,16384]{2,1,0:T(2,128)(2,1)}), bf16[16,2,16384]{2,1,0:T(2,128)(2,1)}, u32[]{:S(2)}, u32[]{:S(2)}) async-start(bf16[16,2,16384]{2,1,0:T(2,128)(2,1)} %reshape.474), calls=%async_computation.5 | async-start | bytes 2097152 | tf_op jit(solution)/shard_map/all_to_all | solution.py:151
  858.5 95.2 %all-to-all-start.4 = ((bf16[16,2,16384]{2,1,0:T(2,128)(2,1)}), bf16[16,2,16384]{2,1,0:T(2,128)(2,1)S(1)}, u32[]{:S(2)}, u32[]{:S(2)}) async-start(bf16[16,2,16384]{2,1,0:T(2,128)(2,1)} %reshape.472), calls=%async_computation.4 | async-start | bytes 2097152 | tf_op jit(solution)/shard_map/all_to_all | solution.py:151
  (170 other events, 1768.2 us)
Sparse Core Ops, SparseCore 0:
  10.7 61.0 all-gather.4
  74.4 55.0 all-gather.6
  222.8 58.4 all-gather.8
  296.6 52.7 all-gather.10
  541.3 64.9 reduce-scatter.19
  653.7 62.0 reduce-scatter.21
  719.3 86.9 reduce-scatter.13
  809.8 84.6 reduce-scatter.17
  898.1 67.2 reduce-scatter.15
where the time goes:
time: 987 us; the launch traced here: 979 us
  matrix products  311 us (32%)
  waiting for transfers between devices  290 us (29%)
  other arithmetic  148 us (15%)
  blocking collectives  93.6 us (9%)
  local copies, waits for them, and re-layouts  72.8 us (7%)
  starting transfers between devices  44.2 us (4%)
  between operations  18.7 us (2%)
    all_gather x4, waiting for transfers between devices, gather_chunk(): own = lax.all_gather(local, 'dp', axis=0, tiled=True)  76.4 us
    ppermute x4, waiting for transfers between devices, reduce_chunk(): arrived = lax.ppermute(other.astype(bf16), 'mx', swap)  76.2 us
    dot_general x4, matrix products, attend_back(): jnp.einsum('qhe,khe->hqk', grad_h, values_h, preferred_element_type=f32)  60.3 us
    pmax x1, blocking collectives, on_device(): lax.pmax(head_rows, chips)  57.6 us
    unnamed x351, local copies, waits for them, and re-layouts  57 us
    ppermute x4, waiting for transfers between devices, gather_chunk(): return (own, lax.ppermute(own, 'mx', swap))  55.1 us
    dot_general x14, matrix products, nn(): lax.dot_general(left, right, (((1,), (0,)), ((), ())), preferred_element_...  50.1 us
    all_to_all x2, waiting for transfers between devices, to_chips(): lax.all_to_all(values, chips, split_axis=0, concat_axis=1, tiled=True)  50.1 us
  transfers between devices with their start and end apart: 36, of which 17 were waited for; matrix products, arithmetic and copies ran while one was open for 43% of the time, Pallas kernels for 0%

commit v1 on v0

--- a/solution.py
+++ b/solution.py
@@ -17,6 +17,12 @@
 chips = ("dp", "mx")
 
 
+def in_order(pieces, dim):
+    dims = list(pieces.shape[1:])
+    dims[dim] *= pieces.shape[0]
+    return jnp.moveaxis(pieces, 0, dim).reshape(dims)
+
+
 def rms_norm(hidden, gain_vec):
     row_scale = lax.rsqrt(jnp.mean(hidden * hidden, axis=-1, keepdims=True) + epsilon)
     return hidden * row_scale * gain_vec
@@ -102,7 +108,19 @@
 
 
 def gather_chunk(local):
-    own = lax.all_gather(local, "dp", axis=0, tiled=True)
+    count = lax.axis_size("dp")
+    pairs = [(i, (i + 1) % count) for i in range(count)]
+    back_2 = [(b_2, a) for a, b_2 in pairs]
+    lower, upper = ([], [])
+    for step in range(count - 1):
+        if step % 2 == 0:
+            lower.append(lax.ppermute(lower[-1] if lower else local, "dp", pairs))
+        else:
+            upper.append(lax.ppermute(upper[-1] if upper else local, "dp", back_2))
+    blocks = jnp.stack([*lower[::-1], local, *upper])
+    shift = lax.axis_index("dp") - len(lower)
+    blocks = blocks[(jnp.arange(count) - shift) % count]
+    own = in_order(blocks, 0)
     return (own, lax.ppermute(own, "mx", swap))
 
 

time: 987 us -> 1070 us (1.084)
  local copies, waits for them, and re-layouts: 72.8 us -> 138 us
  starting transfers between devices: 44.2 us -> 99.7 us
  blocking collectives: 93.6 us -> 61.8 us
    ppermute x0 -> x28, waiting for transfers between devices: none -> 104 us  [the longest x16 66.8 us: gather_chunk(): lower.append(lax.ppermute(lower[-1] if lower else local, 'dp', pairs))]
    all_gather x4 -> x0, waiting for transfers between devices: 76.4 us -> none  [gather_chunk(): own = lax.all_gather(local, 'dp', axis=0, tiled=True)]
    ppermute x0 -> x28, starting transfers between devices: none -> 52.1 us  [the longest x12 33.5 us: gather_chunk(): upper.append(lax.ppermute(upper[-1] if upper else local, 'dp', back_2))]
    all_to_all x2 -> x3, waiting for transfers between devices: 50.1 us -> 0.01 us  [to_chips(): lax.all_to_all(values, chips, split_axis=0, concat_axis=1, tiled=True)]
    unnamed x351 -> x412, local copies, waits for them, and re-layouts: 57 us -> 87 us
    all_to_all x1 -> x0, blocking collectives: 30 us -> none  [to_chips(): lax.all_to_all(values, chips, split_axis=0, concat_axis=1, tiled=True)]
    gather x0 -> x6, local copies, waits for them, and re-layouts: none -> 24.1 us  [gather_chunk(): blocks = blocks[(jnp.arange(count) - shift) % count]]
    ppermute x4, waiting for transfers between devices: 55.1 us -> 70.4 us  [gather_chunk(): return (own, lax.ppermute(own, 'mx', swap))]
  transfers between devices with their start and end apart: 36 -> 61, of which waited for: 17 -> 22; matrix products, arithmetic and copies ran while one was open for 43% -> 46% of each run, Pallas kernels for 0% -> 0%
where the time goes in v1:
time: 1070 us; the launch traced here: 1060 us
  matrix products  307 us (29%)
  waiting for transfers between devices  283 us (26%)
  other arithmetic  152 us (14%)
  local copies, waits for them, and re-layouts  138 us (13%)
  starting transfers between devices  99.7 us (9%)
  blocking collectives  61.8 us (6%)
  between operations  18.9 us (2%)
    unnamed x412, local copies, waits for them, and re-layouts  87 us
    ppermute x4, waiting for transfers between devices, reduce_chunk(): arrived = lax.ppermute(other.astype(bf16), 'mx', swap)  73.8 us
    ppermute x4, waiting for transfers between devices, gather_chunk(): return (own, lax.ppermute(own, 'mx', swap))  70.4 us
    ppermute x16, waiting for transfers between devices, gather_chunk(): lower.append(lax.ppermute(lower[-1] if lower else local, 'dp', pairs))  66.8 us
    dot_general x4, matrix products, attend_back(): jnp.einsum('qhe,khe->hqk', grad_h, values_h, preferred_element_type=f32)  60.4 us
    pmax x1, blocking collectives, on_device(): lax.pmax(head_rows, chips)  55.8 us
    dot_general x14, matrix products, nn(): lax.dot_general(left, right, (((1,), (0,)), ((), ())), preferred_element_...  49.9 us
    convert_element_type x3, other arithmetic, attend_back(): grad_scores = (soft_rows * (grad_soft - row_dot)).astype(bf16)  46.1 us
  transfers between devices with their start and end apart: 61, of which 22 were waited for; matrix products, arithmetic and copies ran while one was open for 46% of the time, Pallas kernels for 0%

profile of v1, /device:TPU:0, one launch (start us, length us, event | category | flops | bytes accessed | tf_op | source)
XLA Modules:
  0.0 1059.8 jit_solution(10537528874189601579)
XLA Ops:
  36.1 28.5 %collective-permute-done.30 = bf16[128,704]{0,1:T(8,128)(2,1)} collective-permute-done((bf16[128,704]{0,1:T(8,128)(2,1)S(1)}, bf16[128,704]{0,1:T(8,128)(2,1)}, u32[]{:S(2)}, u32[]{:S(2)}) %collective-permute-start.30) | collective-permute-done | bytes 180256 | tf_op jit(solution)/shard_map/ppermute | solution.py:117
  82.0 10.1 collective-permute-done.32
  96.7 9.4 collective-permute-done.5
  122.7 14.6 %collective-permute-done.6 = bf16[128,896]{0,1:T(8,128)(2,1)S(1)} collective-permute-done((bf16[128,896]{0,1:T(8,128)(2,1)S(1)}, bf16[128,896]{0,1:T(8,128)(2,1)S(1)}, u32[]{:S(2)}, u32[]{:S(2)}) %collective-permute-start.6) | collective-permute-done | bytes 229408 | tf_op jit(solution)/shard_map/ppermute | solution.py:119
  181.1 12.8 %collective-permute-done.27 = bf16[128,1408]{1,0:T(8,128)(2,1)} collective-permute-done((bf16[128,1408]{1,0:T(8,128)(2,1)S(1)}, bf16[128,1408]{1,0:T(8,128)(2,1)}, u32[]{:S(2)}, u32[]{:S(2)}) %collective-permute-start.27) | collective-permute-done | bytes 360480 | tf_op jit(solution)/shard_map/ppermute | solution.py:119
  197.9 9.4 collective-permute-done.23
  232.6 11.2 %select_reduce_fusion = (f32[4,1024]{1,0:T(4,128)}, f32[4,1024]{1,0:T(4,128)}, f32[4,1024,1024]{1,2,0:T(8,128)}) fusion(pred[1024,1024]{0,1:T(8,128)(4,1)S(1)} %broadcast_compare_fusion, f32[4,1024,1024]{1,2,0:T(8,128)S(1)} %fusion.155, bf16[1024,4,64]{0,2,1:T(8,128)(2,1)} %bitcast.358, bf16[1024,4,64]{0,2,1:T(8,128)(2,1)} %bitcast.356), kind=kOutput, calls=%fused_computation.28 | convolution fusion | flops 553639936 | bytes 35684352 | tf_op jit(solution)/shard_map/qhe,khe->hqk/dot_general | solution.py:62
  243.8 9.1 fusion.1
  259.5 8.3 fusion.78
  267.9 10.6 collective-permute-done.16
  286.8 9.1 collective-permute-done.25
  318.4 8.2 fusion.153
  326.6 8.1 fusion.2
  347.0 8.1 fusion.154
  411.8 40.6 %collective-permute-done.36 = bf16[1024,1408]{1,0:T(8,128)(2,1)} collective-permute-done((bf16[1024,1408]{1,0:T(8,128)(2,1)}, bf16[1024,1408]{1,0:T(8,128)(2,1)}, u32[]{:S(2)}, u32[]{:S(2)}) %collective-permute-start.36) | collective-permute-done | bytes 2883616 | tf_op jit(solution)/shard_map/ppermute | solution.py:124
  463.1 19.2 %collective-permute-done.37 = bf16[1024,704]{0,1:T(8,128)(2,1)} collective-permute-done((bf16[1024,704]{0,1:T(8,128)(2,1)}, bf16[1024,704]{0,1:T(8,128)(2,1)}, u32[]{:S(2)}, u32[]{:S(2)}) %collective-permute-start.37) | collective-permute-done | bytes 1441824 | tf_op jit(solution)/shard_map/ppermute | solution.py:124
  518.9 11.2 %multiply_reduce_fusion.3 = (f32[4,1024]{1,0:T(4,128)}, f32[4,1024,1024]{1,2,0:T(8,128)}) fusion(f32[4,1024,1024]{1,2,0:T(8,128)S(1)} %bitcast.326, f32[4,1024]{1,0:T(4,128)S(1)} %log_add_fusion.3, bf16[1024,4,64]{0,2,1:T(8,128)(2,1)} %bitcast.378, bf16[1024,4,64]{0,2,1:T(8,128)(2,1)} %bitcast.386), kind=kOutput, calls=%fused_computation.14 | convolution fusion | flops 549449728 | bytes 34635776 | tf_op jit(solution)/shard_map/qhe,khe->hqk/dot_general | solution.py:77
  548.1 16.1 %multiply_reduce_fusion.2 = (f32[4,1024]{1,0:T(4,128)}, f32[4,1024,1024]{1,2,0:T(8,128)}) fusion(f32[4,1024,1024]{1,2,0:T(8,128)} %get-tuple-element.99, f32[4,1024]{1,0:T(4,128)S(1)} %copy-done.96, bf16[1024,4,64]{0,2,1:T(8,128)(2,1)} %bitcast.380, bf16[1024,4,64]{0,2,1:T(8,128)(2,1)} %bitcast.384), kind=kOutput, calls=%fused_computation.11 | convolution fusion | flops 549449728 | bytes 34635776 | tf_op jit(solution)/shard_map/qhe,khe->hqk/dot_general | solution.py:77
  564.2 8.4 multiply_convert_fusion.2
  597.2 20.8 %collective-permute-done.49 = bf16[1024,704]{0,1:T(8,128)(2,1)S(1)} collective-permute-done((bf16[1024,704]{0,1:T(8,128)(2,1)S(1)}, bf16[1024,704]{0,1:T(8,128)(2,1)S(1)}, u32[]{:S(2)}, u32[]{:S(2)}) %collective-permute-start.49) | collective-permute-done | bytes 1441824 | tf_op jit(solution)/shard_map/ppermute | solution.py:128
  624.2 8.2 fusion.156
  643.1 8.1 fusion.69
  651.2 24.8 %multiply_reduce_fusion = (f32[4,1024]{1,0:T(4,128)S(1)}, f32[4,1024]{1,0:T(4,128)S(1)}, f32[4,1024,1024]{1,2,0:T(8,128)}) fusion(f32[4,1024,1024]{1,2,0:T(8,128)} %get-tuple-element.95, f32[4,1024]{1,0:T(4,128)S(1)} %log_add_fusion, pred[1024,1024]{0,1:T(8,128)(4,1)S(1)} %copy-done.4, f32[4,1024,1024]{1,2,0:T(8,128)} %fusion.156, ...), kind=kOutput, calls=%fused_computation.5 | convolution fusion | flops 570417152 | bytes 69271552 | tf_op jit(solution)/shard_map/qhe,khe->hqk/dot_general | solution.py:77
  676.0 29.7 %multiply_convert_fusion = (bf16[4,1024,1024]{1,2,0:T(8,128)(2,1)}, bf16[4,1024,1024]{1,2,0:T(8,128)(2,1)}) fusion(f32[4,1024,1024]{1,2,0:T(8,128)} %get-tuple-element.104, f32[4,1024,1024]{1,2,0:T(8,128)} %get-tuple-element.95, f32[4,1024]{1,0:T(4,128)S(1)} %get-tuple-element.31, f32[4,1024]{1,0:T(4,128)S(1)} %log_add_fusion, ...), kind=kLoop, calls=%fused_computation.4 | loop fusion | flops 41943040 | bytes 85000192 | tf_op jit(solution)/shard_map/convert_element_type | solution.py:82
  734.1 8.1 add_convert_fusion
  749.4 8.8 fusion.75
  781.3 31.9 %collective-permute-done.47 = bf16[1024,1024]{0,1:T(8,128)(2,1)} collective-permute-done((bf16[1024,1024]{0,1:T(8,128)(2,1)}, bf16[1024,1024]{0,1:T(8,128)(2,1)}, u32[]{:S(2)}, u32[]{:S(2)}) %collective-permute-start.47) | collective-permute-done | bytes 2097184 | tf_op jit(solution)/shard_map/ppermute | solution.py:128
  838.3 8.2 reduce.10
  860.6 21.1 %collective-permute-done.46 = bf16[1024,1024]{0,1:T(8,128)(2,1)} collective-permute-done((bf16[1024,1024]{0,1:T(8,128)(2,1)}, bf16[1024,1024]{0,1:T(8,128)(2,1)}, u32[]{:S(2)}, u32[]{:S(2)}) %collective-permute-start.46) | collective-permute-done | bytes 2097184 | tf_op jit(solution)/shard_map/ppermute | solution.py:128
  921.0 18.0 %all-to-all-done.5 = bf16[16,2,16384]{2,1,0:T(2,128)(2,1)} async-done(((bf16[16,2,16384]{2,1,0:T(2,128)(2,1)}), bf16[16,2,16384]{2,1,0:T(2,128)(2,1)}, u32[]{:S(2)}, u32[]{:S(2)}) %all-to-all-start.5) | async-done | bytes 1048608 | tf_op jit(solution)/shard_map/all_to_all | solution.py:169
  945.8 55.8 %pmax.7 = f32[2,4]{1,0:T(2,128)S(1)} all-reduce(f32[2,4]{1,0:T(2,128)S(1)} %broadcast_select_fusion.1), channel_id=1, replica_groups=mesh['dp'=8,'mx'=2,'mc'=2] {'dp','mx'}, use_global_device_ids=true, to_apply=%region_22.23 | all-reduce | flops 8 | bytes 64 | tf_op jit(solution)/shard_map/pmax | solution.py:282
  1037.0 9.5 reduce-scatter.16.cloned.1.call-done
  (693 shorter events, 535.2 us)
Async XLA Ops:
  8.9 109.1 %collective-permute-start.33 = (bf16[128,704]{0,1:T(8,128)(2,1)}, bf16[128,704]{0,1:T(8,128)(2,1)}, u32[]{:S(2)}, u32[]{:S(2)}) collective-permute-start(bf16[128,704]{0,1:T(8,128)(2,1)} %convert_bitcast_fusion.2), channel_id=1, source_target_pairs={{4,0},{8,4},{12,8},{16,12},{20,16},{24,20},{28,24},{0,28},{5,1},{9... | collective-permute-start | bytes 540680 | tf_op jit(solution)/shard_map/ppermute | solution.py:119
  18.6 56.8 %collective-permute-start.4 = (bf16[128,896]{0,1:T(8,128)(2,1)}, bf16[128,896]{0,1:T(8,128)(2,1)}, u32[]{:S(2)}, u32[]{:S(2)}) collective-permute-start(bf16[128,896]{0,1:T(8,128)(2,1)} %maximum_maximum_fusion), channel_id=1, source_target_pairs={{4,0},{8,4},{12,8},{16,12},{20,16},{24,20},{28,24},{0,28},{5,1},{9... | collective-permute-start | bytes 688136 | tf_op jit(solution)/shard_map/ppermute | solution.py:119
  23.3 138.8 %all-to-all-start = ((bf16[16,32,1024]{2,1,0:T(8,128)(2,1)}), bf16[16,32,1024]{2,1,0:T(8,128)(2,1)S(1)}, u32[]{:S(2)}, u32[]{:S(2)}) async-start(bf16[16,32,1024]{2,1,0:T(8,128)(2,1)} %param.20), calls=%async_computation | async-start | bytes 2097152 | tf_op jit(solution)/shard_map/all_to_all | solution.py:165
  31.2 48.8 %collective-permute-start.8 = (bf16[128,1280]{0,1:T(8,128)(2,1)}, bf16[128,1280]{0,1:T(8,128)(2,1)}, u32[]{:S(2)}, u32[]{:S(2)}) collective-permute-start(bf16[128,1280]{0,1:T(8,128)(2,1)} %pad_maximum_fusion.27), channel_id=1, source_target_pairs={{0,4},{4,8},{8,12},{12,16},{16,20},{20,24},{24,28},{28,0},{1,5},{5... | collective-permute-start | bytes 983048 | tf_op jit(solution)/shard_map/ppermute | solution.py:117
  75.4 45.5 %collective-permute-start.12 = (bf16[128,1280]{0,1:T(8,128)(2,1)}, bf16[128,1280]{0,1:T(8,128)(2,1)}, u32[]{:S(2)}, u32[]{:S(2)}) collective-permute-start(bf16[128,1280]{0,1:T(8,128)(2,1)} %pad_maximum_fusion.27), channel_id=1, source_target_pairs={{4,0},{8,4},{12,8},{16,12},{20,16},{24,20},{28,24},{0,28},{5,1},{9... | collective-permute-start | bytes 983048 | tf_op jit(solution)/shard_map/ppermute | solution.py:119
  106.1 63.9 %collective-permute-start.26 = (bf16[128,1408]{1,0:T(8,128)(2,1)}, bf16[128,1408]{1,0:T(8,128)(2,1)S(1)}, u32[]{:S(2)}, u32[]{:S(2)}) collective-permute-start(bf16[128,1408]{1,0:T(8,128)(2,1)} %copy.162), channel_id=1, source_target_pairs={{4,0},{8,4},{12,8},{16,12},{20,16},{24,20},{28,24},{0,28},{5,1},{9... | collective-permute-start | bytes 1081352 | tf_op jit(solution)/shard_map/ppermute | solution.py:119
  106.2 39.1 %collective-permute-start.10 = (bf16[128,1280]{0,1:T(8,128)(2,1)S(1)}, bf16[128,1280]{0,1:T(8,128)(2,1)}, u32[]{:S(2)}, u32[]{:S(2)}) collective-permute-start(bf16[128,1280]{0,1:T(8,128)(2,1)S(1)} %collective-permute-done.9), channel_id=1, source_target_pairs={{0,4},{4,8},{8,12},{12,16},{16,20},{20,24},{24,28},{28,0},{1,5},{5... | collective-permute-start | bytes 983048 | tf_op jit(solution)/shard_map/ppermute | solution.py:117
  118.0 56.6 %collective-permute-start.22 = (bf16[128,1408]{1,0:T(8,128)(2,1)}, bf16[128,1408]{1,0:T(8,128)(2,1)}, u32[]{:S(2)}, u32[]{:S(2)}) collective-permute-start(bf16[128,1408]{1,0:T(8,128)(2,1)} %copy.162), channel_id=1, source_target_pairs={{0,4},{4,8},{8,12},{12,16},{16,20},{20,24},{24,28},{28,0},{1,5},{5... | collective-permute-start | bytes 1081352 | tf_op jit(solution)/shard_map/ppermute | solution.py:117
  120.9 47.3 %collective-permute-start.34 = (bf16[128,704]{0,1:T(8,128)(2,1)}, bf16[128,704]{0,1:T(8,128)(2,1)S(1)}, u32[]{:S(2)}, u32[]{:S(2)}) collective-permute-start(bf16[128,704]{0,1:T(8,128)(2,1)} %collective-permute-done.33), channel_id=1, source_target_pairs={{4,0},{8,4},{12,8},{16,12},{20,16},{24,20},{28,24},{0,28},{5,1},{9... | collective-permute-start | bytes 540680 | tf_op jit(solution)/shard_map/ppermute | solution.py:119
  155.3 69.5 %collective-permute-start.15 = (bf16[1024,896]{1,0:T(8,128)(2,1)}, bf16[1024,896]{1,0:T(8,128)(2,1)}, u32[]{:S(2)}, u32[]{:S(2)}) collective-permute-start(bf16[1024,896]{1,0:T(8,128)(2,1)} %bitcast.375), channel_id=1, source_target_pairs={{0,2},{2,0},{1,3},{3,1},{4,6},{6,4},{5,7},{7,5},{8,10},{10,8},{9,1... | collective-permute-start | bytes 5505032 | tf_op jit(solution)/shard_map/ppermute | solution.py:124
  162.2 136.3 %all-to-all-start.1 = ((bf16[16,32,1024]{2,1,0:T(8,128)(2,1)}), bf16[16,32,1024]{2,1,0:T(8,128)(2,1)}, u32[]{:S(2)}, u32[]{:S(2)}) async-start(bf16[16,32,1024]{2,1,0:T(8,128)(2,1)} %param.21), calls=%async_computation.1 | async-start | bytes 2097152 | tf_op jit(solution)/shard_map/all_to_all | solution.py:165
  168.2 51.7 %collective-permute-start.7 = (bf16[512,1024]{1,0:T(8,128)(2,1)}, bf16[512,1024]{1,0:T(8,128)(2,1)}, u32[]{:S(2)}, u32[]{:S(2)}) collective-permute-start(bf16[512,1024]{1,0:T(8,128)(2,1)} %fusion.52), channel_id=1, source_target_pairs={{0,1},{1,0},{2,3},{3,2},{4,5},{5,4},{6,7},{7,6},{8,9},{9,8},{10,11... | collective-permute-start | bytes 3145736 | tf_op jit(solution)/shard_map/ppermute | solution.py:48
  193.9 202.3 %collective-permute-start.35 = (bf16[128,704]{0,1:T(8,128)(2,1)}, bf16[128,704]{0,1:T(8,128)(2,1)}, u32[]{:S(2)}, u32[]{:S(2)}) collective-permute-start(bf16[128,704]{0,1:T(8,128)(2,1)} %copy-done.106), channel_id=1, source_target_pairs={{4,0},{8,4},{12,8},{16,12},{20,16},{24,20},{28,24},{0,28},{5,1},{9... | collective-permute-start | bytes 540680 | tf_op jit(solution)/shard_map/ppermute | solution.py:119
  207.3 173.3 %collective-permute-start.28 = (bf16[128,1408]{1,0:T(8,128)(2,1)}, bf16[128,1408]{1,0:T(8,128)(2,1)}, u32[]{:S(2)}, u32[]{:S(2)}) collective-permute-start(bf16[128,1408]{1,0:T(8,128)(2,1)} %collective-permute-done.27), channel_id=1, source_target_pairs={{4,0},{8,4},{12,8},{16,12},{20,16},{24,20},{28,24},{0,28},{5,1},{9... | collective-permute-start | bytes 1081352 | tf_op jit(solution)/shard_map/ppermute | solution.py:119
  210.0 72.8 %collective-permute-start.24 = (bf16[128,1408]{1,0:T(8,128)(2,1)}, bf16[128,1408]{1,0:T(8,128)(2,1)}, u32[]{:S(2)}, u32[]{:S(2)}) collective-permute-start(bf16[128,1408]{1,0:T(8,128)(2,1)} %collective-permute-done.23), channel_id=1, source_target_pairs={{0,4},{4,8},{8,12},{12,16},{16,20},{20,24},{24,28},{28,0},{1,5},{5... | collective-permute-start | bytes 1081352 | tf_op jit(solution)/shard_map/ppermute | solution.py:117
  219.9 58.6 %collective-permute-start.16 = (bf16[1024,1280]{1,0:T(8,128)(2,1)}, bf16[1024,1280]{1,0:T(8,128)(2,1)}, u32[]{:S(2)}, u32[]{:S(2)}) collective-permute-start(bf16[1024,1280]{1,0:T(8,128)(2,1)} %bitcast.339), channel_id=1, source_target_pairs={{0,2},{2,0},{1,3},{3,1},{4,6},{6,4},{5,7},{7,5},{8,10},{10,8},{9,1... | collective-permute-start | bytes 7864328 | tf_op jit(solution)/shard_map/ppermute | solution.py:124
  298.4 105.7 %all-to-all-start.3 = ((bf16[16,32,1024]{2,1,0:T(8,128)(2,1)}), bf16[16,32,1024]{2,1,0:T(8,128)(2,1)}, u32[]{:S(2)}, u32[]{:S(2)}) async-start(bf16[16,32,1024]{2,1,0:T(8,128)(2,1)} %param.22), calls=%async_computation.3 | async-start | bytes 2097152 | tf_op jit(solution)/shard_map/all_to_all | solution.py:165
  302.8 705.7 %reduce-scatter.20.cloned.1.call-start = ((), (), s32[]{:S(2)}) async-start(), calls=%async_computation.14 | async-start | bytes 1769472
  386.8 65.7 %collective-permute-start.36 = (bf16[1024,1408]{1,0:T(8,128)(2,1)}, bf16[1024,1408]{1,0:T(8,128)(2,1)}, u32[]{:S(2)}, u32[]{:S(2)}) collective-permute-start(bf16[1024,1408]{1,0:T(8,128)(2,1)} %bitcast.371), channel_id=1, source_target_pairs={{0,2},{2,0},{1,3},{3,1},{4,6},{6,4},{5,7},{7,5},{8,10},{10,8},{9,1... | collective-permute-start | bytes 8650760 | tf_op jit(solution)/shard_map/ppermute | solution.py:124
  403.8 78.6 %collective-permute-start.37 = (bf16[1024,704]{0,1:T(8,128)(2,1)}, bf16[1024,704]{0,1:T(8,128)(2,1)}, u32[]{:S(2)}, u32[]{:S(2)}) collective-permute-start(bf16[1024,704]{0,1:T(8,128)(2,1)} %copy_bitcast_fusion), channel_id=1, source_target_pairs={{0,2},{2,0},{1,3},{3,1},{4,6},{6,4},{5,7},{7,5},{8,10},{10,8},{9,1... | collective-permute-start | bytes 4325384 | tf_op jit(solution)/shard_map/ppermute | solution.py:124
  405.6 52.7 %collective-permute-start.39 = (bf16[512,1024]{1,0:T(8,128)(2,1)S(1)}, bf16[512,1024]{1,0:T(8,128)(2,1)S(1)}, u32[]{:S(2)}, u32[]{:S(2)}) collective-permute-start(bf16[512,1024]{1,0:T(8,128)(2,1)S(1)} %fusion.47), channel_id=1, source_target_pairs={{0,1},{1,0},{2,3},{3,2},{4,5},{5,4},{6,7},{7,6},{8,9},{9,8},{10,11... | collective-permute-start | bytes 3145736 | tf_op jit(solution)/shard_map/ppermute | solution.py:48
  596.4 137.7 %collective-permute-start.48 = (bf16[1024,1408]{1,0:T(8,128)(2,1)}, bf16[1024,1408]{1,0:T(8,128)(2,1)}, u32[]{:S(2)}, u32[]{:S(2)}) collective-permute-start(bf16[1024,1408]{1,0:T(8,128)(2,1)} %convolution_convert_fusion), channel_id=1, source_target_pairs={{0,2},{2,0},{1,3},{3,1},{4,6},{6,4},{5,7},{7,5},{8,10},{10,8},{9,1... | collective-permute-start | bytes 8650760 | tf_op jit(solution)/shard_map/ppermute | solution.py:128
  621.5 396.6 %reduce-scatter.22.cloned.1.call-start = ((), (), s32[]{:S(2)}) async-start(), calls=%async_computation.15 | async-start | bytes 589824
  733.6 292.0 %reduce-scatter.14.cloned.1.call-start = ((), (), s32[]{:S(2)}) async-start(), calls=%async_computation.11 | async-start | bytes 3244032 | tf_op jit(solution)/shard_map/reduce_scatter | solution.py:130
  742.3 289.7 %reduce-scatter.18.cloned.1.call-start = ((), (), s32[]{:S(2)}) async-start(), calls=%async_computation.13 | async-start | bytes 2359296
  765.2 48.0 %collective-permute-start.47 = (bf16[1024,1024]{0,1:T(8,128)(2,1)}, bf16[1024,1024]{0,1:T(8,128)(2,1)}, u32[]{:S(2)}, u32[]{:S(2)}) collective-permute-start(bf16[1024,1024]{0,1:T(8,128)(2,1)} %pad_maximum_fusion.10), channel_id=1, source_target_pairs={{0,2},{2,0},{1,3},{3,1},{4,6},{6,4},{5,7},{7,5},{8,10},{10,8},{9,1... | collective-permute-start | bytes 6291464 | tf_op jit(solution)/shard_map/ppermute | solution.py:128
  828.2 53.5 %collective-permute-start.46 = (bf16[1024,1024]{0,1:T(8,128)(2,1)}, bf16[1024,1024]{0,1:T(8,128)(2,1)}, u32[]{:S(2)}, u32[]{:S(2)}) collective-permute-start(bf16[1024,1024]{0,1:T(8,128)(2,1)} %pad_maximum_fusion.9), channel_id=1, source_target_pairs={{0,2},{2,0},{1,3},{3,1},{4,6},{6,4},{5,7},{7,5},{8,10},{10,8},{9,1... | collective-permute-start | bytes 6291464 | tf_op jit(solution)/shard_map/ppermute | solution.py:128
  836.0 50.8 %collective-permute-start.45 = (f32[512,1024]{1,0:T(8,128)}, f32[512,1024]{1,0:T(8,128)}, u32[]{:S(2)}, u32[]{:S(2)}) collective-permute-start(f32[512,1024]{1,0:T(8,128)} %slice.258), channel_id=1, source_target_pairs={{0,1},{1,0},{2,3},{3,2},{4,5},{5,4},{6,7},{7,6},{8,9},{9,8},{10,11... | collective-permute-start | bytes 6291464 | tf_op jit(solution)/shard_map/ppermute | solution.py:53
  849.1 52.3 %all-to-all-start.2 = ((bf16[16,2,16384]{2,1,0:T(2,128)(2,1)}), bf16[16,2,16384]{2,1,0:T(2,128)(2,1)}, u32[]{:S(2)}, u32[]{:S(2)}) async-start(bf16[16,2,16384]{2,1,0:T(2,128)(2,1)} %reshape.570), calls=%async_computation.2 | async-start | bytes 2097152 | tf_op jit(solution)/shard_map/all_to_all | solution.py:169
  854.8 191.6 %reduce-scatter.16.cloned.1.call-start = ((), (), s32[]{:S(2)}) async-start(), calls=%async_computation.12 | async-start | bytes 2359296
  901.5 37.5 %all-to-all-start.5 = ((bf16[16,2,16384]{2,1,0:T(2,128)(2,1)}), bf16[16,2,16384]{2,1,0:T(2,128)(2,1)}, u32[]{:S(2)}, u32[]{:S(2)}) async-start(bf16[16,2,16384]{2,1,0:T(2,128)(2,1)} %reshape.574), calls=%async_computation.5 | async-start | bytes 2097152 | tf_op jit(solution)/shard_map/all_to_all | solution.py:169
  939.0 95.1 %all-to-all-start.4 = ((bf16[16,2,16384]{2,1,0:T(2,128)(2,1)}), bf16[16,2,16384]{2,1,0:T(2,128)(2,1)S(1)}, u32[]{:S(2)}, u32[]{:S(2)}) async-start(bf16[16,2,16384]{2,1,0:T(2,128)(2,1)} %reshape.572), calls=%async_computation.4 | async-start | bytes 2097152 | tf_op jit(solution)/shard_map/all_to_all | solution.py:169
  (213 other events, 2877.6 us)
Sparse Core Ops, SparseCore 0:
  621.6 65.9 reduce-scatter.19
  733.7 62.9 reduce-scatter.21
  800.3 87.3 reduce-scatter.13
  891.1 84.5 reduce-scatter.17
  979.1 67.3 reduce-scatter.15
